TPU v7x, 128 devices: a whole 4x4x4 slice. The times are simulated.
128 devices in a mesh: band: 8 (over y, z_hi), plane: 16 (over z_lo, x, core).
Axes of the slice: x: 4, y: 4, z: 4 (z_hi: 2, z_lo: 2; z = z_hi * 2 + z_lo), core: 2. Of those that a mesh axis runs over, the one named last changes fastest.
Arguments:
- orbitals: float32 [64, 96, 9216], P('band', 'plane'), may hold values from -6 to 6
Outputs:
- exchange_action: float32 [64, 96, 9216], P('band', 'plane')
All inputs are finite; a program needn't handle non-finite values.
Results may differ from a plain program's by a relative error of at most 0.0001.
Values sent between devices are 32-bit elements; how exact they have to be, the bound alone decides.
A program may use at most 128 MiB of HBM per device.

v0:
```python
import math
import jax
import jax.numpy as jnp
from jax import lax
from jax.sharding import PartitionSpec as P

PAIR = 2
ROUNDS = 4
OMEGA = 0.106
CELL = 41.05
ALPHA = 0.25
HIGHEST = lax.Precision.HIGHEST


def from_root(value, axis, source):
    kept = jnp.where(lax.axis_index(axis) == source, value, 0).astype(value.dtype)
    return lax.psum(kept, axis)


def hartley_table(count):
    index = jnp.arange(count, dtype=jnp.int32)
    product = index[:, None] * index[None, :] % count
    angle = product.astype(jnp.float32) * (2.0 * math.pi / count)
    return jnp.cos(angle) + jnp.sin(angle)


def frequencies(count):
    index = jnp.arange(count, dtype=jnp.int32)
    return jnp.where(index <= count // 2, index, index - count).astype(jnp.float32)


def screened_kernel(count, first, width):
    freq = frequencies(count)
    square = freq * freq
    middle = lax.dynamic_slice_in_dim(square, first, width)
    scale = (2.0 * math.pi / CELL) ** 2
    g_two = scale * (square[:, None, None] + middle[None, :, None] + square[None, None, :])
    positive = g_two > 0
    safe = jnp.where(positive, g_two, 1.0)
    value = 4.0 * math.pi / safe * -jnp.expm1(-safe / (4.0 * OMEGA * OMEGA))
    value = jnp.where(positive, value, math.pi / (OMEGA * OMEGA))
    return value / float(count**3)


def coulomb_solve(density, table, kernel):
    field = jnp.einsum("pxyz,zw->pxyw", density, table, precision=HIGHEST)
    field = jnp.einsum("pxyz,yv->pxvz", field, table, precision=HIGHEST)
    field = lax.all_to_all(field, "plane", split_axis=2, concat_axis=1, tiled=True)
    field = jnp.einsum("pxyz,xu->puyz", field, table, precision=HIGHEST) * kernel
    field = jnp.einsum("pxyz,xu->puyz", field, table, precision=HIGHEST)
    field = lax.all_to_all(field, "plane", split_axis=1, concat_axis=2, tiled=True)
    field = jnp.einsum("pxyz,zw->pxyw", field, table, precision=HIGHEST)
    return jnp.einsum("pxyz,yv->pxvz", field, table, precision=HIGHEST)


def fetch_pair(fields, turn):
    return from_root(fields[0:PAIR], "band", turn)


def local(orbitals):
    local_bands, planes, flat = orbitals.shape
    count = planes * lax.axis_size("plane")
    fields = orbitals.reshape(local_bands, planes, count, count)
    table = hartley_table(count)
    kernel = screened_kernel(count, lax.axis_index("plane") * planes, planes)
    shape_tail = (planes, count, count)
    local_sum = jnp.zeros_like(fields)
    owner_list = []
    for turn in range(ROUNDS):
        received = fetch_pair(fields, turn)
        density = (fields[:, None] * received[None]).reshape((local_bands * PAIR,) + shape_tail)
        potential = coulomb_solve(density, table, kernel).reshape((local_bands, PAIR) + shape_tail)
        local_sum = local_sum + jnp.sum(received[None] * potential, axis=1)
        owner_list.append(jnp.sum(fields[:, None] * potential, axis=0))
    owner_terms = jnp.stack(owner_list)
    own_extra = jnp.zeros((PAIR,) + shape_tail, jnp.float32)
    for turn in range(ROUNDS):
        summed = lax.psum(owner_terms[turn], "band")
        owner_flag = (lax.axis_index("band") == turn).astype(jnp.float32)
        own_extra = own_extra + owner_flag * summed
    local_sum = local_sum.at[0:PAIR].add(own_extra)
    return (-ALPHA * local_sum).reshape(local_bands, planes, count * count)


def solution(mesh):
    placed = (P("band", "plane", None),)
    return jax.shard_map(
        local, mesh=mesh, in_specs=placed, out_specs=P("band", "plane", None), check_vma=False
    )
```

profile of v0, /device:TPU:8, one launch (start us, length us, event | category | flops | bytes accessed | tf_op | source)
XLA Modules:
  0.0 886.8 jit_solution(3193934926200104955)
XLA Ops:
  13.7 2.4 mul.424
  16.1 122.7 %all-reduce.7.cloned.1.call-done = (f32[2,6,96,96]{3,2,0,1:T(8,128)}, f32[2,6,96,96]{3,2,0,1:T(8,128)}, f32[2,6,96,96]{3,2,0,1:T(8,128)}, f32[2,6,96,96]{3,2,0,1:T(8,128)}) async-done(((f32[2,6,96,96]{3,2,0,1:T(8,128)}, f32[2,6,96,96]{3,2,0,1:T(8,128)}, f32[2,6,96,96]{3,2,0,1:T(8,128)}, f32[2,6,96,96]{3,2,0,1:T(8,128)}), (f32[2,6,96,96]{3,2,0,1:T(8,128)}, f32[2,6,96,96]{3,2,0,1:T(8,128)}, ...) | async-done | bytes 1769488 | tf_op jit(solution)/shard_map/psum | solution.py:17
  138.8 9.3 %broadcast_multiply_fusion.2 = (f32[8,2,6,96,96]{4,3,2,1,0:T(8,128)}, f32[8,2,6,96,96]{4,3,2,1,0:T(8,128)}, f32[8,2,6,96,96]{4,3,2,1,0:T(8,128)}, f32[8,2,6,96,96]{4,3,2,1,0:T(8,128)}) fusion(f32[2,6,96,96]{3,2,0,1:T(8,128)} %get-tuple-element.27, f32[2,6,96,96]{3,2,0,1:T(8,128)} %get-tuple-element.26, f32[8,6,96,96]{3,2,0,1:T(8,128)S(1)} %mul.424, ...), kind=kLoop, calls=%fused_computation.39 | loop fusion | flops 3538944 | bytes 17694720 | tf_op jit(solution)/shard_map/mul | solution.py:71
  148.1 6.3 fusion.52
  154.4 4.5 convolution_bitcast_fusion.1
  158.9 4.9 copy.143
  163.8 4.8 all-to-all-start.4
  168.6 6.3 fusion.55
  175.0 4.5 convolution_bitcast_fusion.2
  179.5 4.9 copy.133
  184.4 47.5 %all-to-all-done.4 = f32[16,6,96,96]{3,0,1,2:T(8,128)} async-done(((f32[16,6,96,96]{3,0,1,2:T(8,128)}), f32[16,6,96,96]{3,0,1,2:T(8,128)}, u32[]{:S(2)}, u32[]{:S(2)}) %all-to-all-start.4) | async-done | bytes 3538976 | tf_op jit(solution)/shard_map/all_to_all | solution.py:48
  231.9 5.1 all-to-all-start.2
  237.1 6.3 fusion.49
  243.4 4.5 convolution_bitcast_fusion
  247.9 4.9 copy.153
  252.9 47.7 %all-to-all-done.2 = f32[16,6,96,96]{3,0,1,2:T(8,128)} async-done(((f32[16,6,96,96]{3,0,1,2:T(8,128)}), f32[16,6,96,96]{3,0,1,2:T(8,128)}, u32[]{:S(2)}, u32[]{:S(2)}) %all-to-all-start.2) | async-done | bytes 3538976 | tf_op jit(solution)/shard_map/all_to_all | solution.py:48
  300.6 4.7 all-to-all-start.6
  305.3 6.3 fusion.58
  311.7 4.5 convolution_bitcast_fusion.3
  316.2 4.9 copy.123
  321.1 47.7 %all-to-all-done.6 = f32[16,6,96,96]{3,0,1,2:T(8,128)} async-done(((f32[16,6,96,96]{3,0,1,2:T(8,128)}), f32[16,6,96,96]{3,0,1,2:T(8,128)}, u32[]{:S(2)}, u32[]{:S(2)}) %all-to-all-start.6) | async-done | bytes 3538976 | tf_op jit(solution)/shard_map/all_to_all | solution.py:48
  368.8 5.0 all-to-all-start
  374.2 2.9 copy.145
  377.1 7.1 fusion.14
  384.2 4.7 fusion.38
  389.0 4.9 copy.147
  393.9 42.9 %all-to-all-done = f32[16,6,96,96]{3,0,1,2:T(8,128)} async-done(((f32[16,6,96,96]{3,0,1,2:T(8,128)}), f32[16,6,96,96]{3,0,1,2:T(8,128)}, u32[]{:S(2)}, u32[]{:S(2)}) %all-to-all-start) | async-done | bytes 3538976 | tf_op jit(solution)/shard_map/all_to_all | solution.py:48
  436.8 4.6 all-to-all-start.5
  441.4 2.9 copy.135
  444.3 7.1 fusion.18
  451.5 5.0 fusion.35
  456.4 4.9 copy.137
  461.4 43.5 %all-to-all-done.5 = f32[16,96,6,96]{3,0,2,1:T(8,128)} async-done(((f32[16,96,6,96]{3,0,2,1:T(8,128)}), f32[16,96,6,96]{3,0,2,1:T(8,128)}, u32[]{:S(2)}, u32[]{:S(2)}) %all-to-all-start.5) | async-done | bytes 3538976 | tf_op jit(solution)/shard_map/all_to_all | solution.py:51
  504.9 4.6 all-to-all-start.3
  509.5 2.9 copy.155
  512.4 7.1 fusion.10
  519.5 4.7 fusion.41
  524.3 4.9 copy.157
  529.1 43.8 %all-to-all-done.3 = f32[16,96,6,96]{3,0,2,1:T(8,128)} async-done(((f32[16,96,6,96]{3,0,2,1:T(8,128)}), f32[16,96,6,96]{3,0,2,1:T(8,128)}, u32[]{:S(2)}, u32[]{:S(2)}) %all-to-all-start.3) | async-done | bytes 3538976 | tf_op jit(solution)/shard_map/all_to_all | solution.py:51
  572.9 4.6 all-to-all-start.7
  577.5 2.9 copy.125
  580.4 7.4 fusion.22
  587.8 5.3 fusion.32
  593.2 5.0 copy.127
  598.1 42.9 %all-to-all-done.7 = f32[16,96,6,96]{3,0,2,1:T(8,128)} async-done(((f32[16,96,6,96]{3,0,2,1:T(8,128)}), f32[16,96,6,96]{3,0,2,1:T(8,128)}, u32[]{:S(2)}, u32[]{:S(2)}) %all-to-all-start.7) | async-done | bytes 3538976 | tf_op jit(solution)/shard_map/all_to_all | solution.py:51
  641.1 4.6 all-to-all-start.1
  650.4 2.8 copy.148
  653.2 2.8 copy.138
  656.0 2.8 copy.158
  658.8 7.0 fusion.12
  665.7 7.0 fusion.16
  672.7 7.0 fusion.8
  679.8 29.3 %all-to-all-done.1 = f32[16,96,6,96]{3,0,2,1:T(8,128)} async-done(((f32[16,96,6,96]{3,0,2,1:T(8,128)}), f32[16,96,6,96]{3,0,2,1:T(8,128)}, u32[]{:S(2)}, u32[]{:S(2)}) %all-to-all-start.1) | async-done | bytes 3538976 | tf_op jit(solution)/shard_map/all_to_all | solution.py:51
  709.1 2.8 copy.128
  711.9 5.4 fusion.20
  717.4 6.3 multiply_reduce_fusion.6
  723.7 6.6 multiply_reduce_fusion.5
  730.3 6.6 multiply_reduce_fusion.4
  736.9 6.8 multiply_reduce_fusion.7
  743.6 5.3 multiply_reduce_fusion.3
  748.9 4.8 add_add_fusion
  753.7 117.3 %all-reduce.5.cloned.1.call-done = (f32[2,6,96,96]{3,2,1,0:T(8,128)}, f32[2,6,96,96]{3,2,1,0:T(8,128)}, f32[2,6,96,96]{3,2,1,0:T(8,128)}, f32[2,6,96,96]{3,2,1,0:T(8,128)}) async-done(((f32[2,6,96,96]{3,2,1,0:T(8,128)}, f32[2,6,96,96]{3,2,1,0:T(8,128)}, f32[2,6,96,96]{3,2,1,0:T(8,128)}, f32[2,6,96,96]{3,2,1,0:T(8,128)}), (f32[2,6,96,96]{3,2,1,0:T(8,128)}, f32[2,6,96,96]{3,2,1,0:T(8,128)}, ...) | async-done | bytes 1769488 | tf_op jit(solution)/shard_map/psum | solution.py:78
  874.7 2.7 reshape.164
  877.4 2.2 copy.183
  (44 shorter events, 16.0 us)
Async XLA Ops:
  6.5 132.2 %all-reduce.7.cloned.1.call-start = ((), (), s32[]{:S(2)}) async-start(), calls=%async_computation.9 | async-start | bytes 4718592 | tf_op jit(solution)/shard_map/psum | solution.py:17
  163.8 68.1 %all-to-all-start.4 = ((f32[16,6,96,96]{3,0,1,2:T(8,128)}), f32[16,6,96,96]{3,0,1,2:T(8,128)}, u32[]{:S(2)}, u32[]{:S(2)}) async-start(f32[16,6,96,96]{3,0,1,2:T(8,128)} %copy.143), calls=%async_computation.4 | async-start | bytes 9437184 | tf_op jit(solution)/shard_map/all_to_all | solution.py:48
  231.9 68.6 %all-to-all-start.2 = ((f32[16,6,96,96]{3,0,1,2:T(8,128)}), f32[16,6,96,96]{3,0,1,2:T(8,128)}, u32[]{:S(2)}, u32[]{:S(2)}) async-start(f32[16,6,96,96]{3,0,1,2:T(8,128)} %copy.133), calls=%async_computation.2 | async-start | bytes 9437184 | tf_op jit(solution)/shard_map/all_to_all | solution.py:48
  300.6 68.2 %all-to-all-start.6 = ((f32[16,6,96,96]{3,0,1,2:T(8,128)}), f32[16,6,96,96]{3,0,1,2:T(8,128)}, u32[]{:S(2)}, u32[]{:S(2)}) async-start(f32[16,6,96,96]{3,0,1,2:T(8,128)} %copy.153), calls=%async_computation.6 | async-start | bytes 9437184 | tf_op jit(solution)/shard_map/all_to_all | solution.py:48
  368.8 68.1 %all-to-all-start = ((f32[16,6,96,96]{3,0,1,2:T(8,128)}), f32[16,6,96,96]{3,0,1,2:T(8,128)}, u32[]{:S(2)}, u32[]{:S(2)}) async-start(f32[16,6,96,96]{3,0,1,2:T(8,128)} %copy.123), calls=%async_computation | async-start | bytes 9437184 | tf_op jit(solution)/shard_map/all_to_all | solution.py:48
  436.8 68.0 %all-to-all-start.5 = ((f32[16,96,6,96]{3,0,2,1:T(8,128)}), f32[16,96,6,96]{3,0,2,1:T(8,128)}, u32[]{:S(2)}, u32[]{:S(2)}) async-start(f32[16,96,6,96]{3,0,2,1:T(8,128)} %copy.147), calls=%async_computation.5 | async-start | bytes 9437184 | tf_op jit(solution)/shard_map/all_to_all | solution.py:51
  504.9 68.0 %all-to-all-start.3 = ((f32[16,96,6,96]{3,0,2,1:T(8,128)}), f32[16,96,6,96]{3,0,2,1:T(8,128)}, u32[]{:S(2)}, u32[]{:S(2)}) async-start(f32[16,96,6,96]{3,0,2,1:T(8,128)} %copy.137), calls=%async_computation.3 | async-start | bytes 9437184 | tf_op jit(solution)/shard_map/all_to_all | solution.py:51
  572.9 68.1 %all-to-all-start.7 = ((f32[16,96,6,96]{3,0,2,1:T(8,128)}), f32[16,96,6,96]{3,0,2,1:T(8,128)}, u32[]{:S(2)}, u32[]{:S(2)}) async-start(f32[16,96,6,96]{3,0,2,1:T(8,128)} %copy.157), calls=%async_computation.7 | async-start | bytes 9437184 | tf_op jit(solution)/shard_map/all_to_all | solution.py:51
  598.1 51.4 %copy-start.1 = (f32[2,6,96,96]{3,2,0,1:T(8,128)S(1)}, f32[2,6,96,96]{3,2,0,1:T(8,128)}, u32[]{:S(2)}) copy-start(f32[2,6,96,96]{3,2,0,1:T(8,128)} %get-tuple-element.27) | copy-start | bytes 1327108
  598.1 52.2 %copy-start = (f32[2,6,96,96]{3,2,0,1:T(8,128)S(1)}, f32[2,6,96,96]{3,2,0,1:T(8,128)}, u32[]{:S(2)}) copy-start(f32[2,6,96,96]{3,2,0,1:T(8,128)} %get-tuple-element.28) | copy-start | bytes 1327108
  641.1 68.0 %all-to-all-start.1 = ((f32[16,96,6,96]{3,0,2,1:T(8,128)}), f32[16,96,6,96]{3,0,2,1:T(8,128)}, u32[]{:S(2)}, u32[]{:S(2)}) async-start(f32[16,96,6,96]{3,0,2,1:T(8,128)} %copy.127), calls=%async_computation.1 | async-start | bytes 9437184 | tf_op jit(solution)/shard_map/all_to_all | solution.py:51
  645.6 225.4 %all-reduce.5.cloned.1.call-start = ((), (), s32[]{:S(2)}) async-start(), calls=%async_computation.8 | async-start | bytes 4718592 | tf_op jit(solution)/shard_map/psum | solution.py:78
  709.1 8.3 slice-start.4
  711.9 5.4 slice-start.5
  711.9 11.8 %slice-start.2 = ((s8[4718592]{0:T(1024)(128)(4,1)}), s8[4194304]{0:T(1024)(128)(4,1)S(1)}, s32[]{:S(2)}) async-start(s8[4718592]{0:T(1024)(128)(4,1)} %bitcast.181), calls=%async_computation.12 | async-start | bytes 8388608
  717.3 6.3 slice-start.3
  717.4 6.3 copy-start.4
  717.4 12.9 %slice-start = ((s8[4718592]{0:T(1024)(128)(4,1)}), s8[4194304]{0:T(1024)(128)(4,1)S(1)}, s32[]{:S(2)}) async-start(s8[4718592]{0:T(1024)(128)(4,1)} %bitcast.179), calls=%async_computation.10 | async-start | bytes 8388608
  723.7 6.6 slice-start.1
  723.7 6.6 copy-start.3
  730.3 6.6 copy-start.2
Sparse Core Ops, SparseCore 0:
  13.8 124.9 all-reduce.6
  749.0 121.9 all-reduce.4
where the time goes:
time: 890 us; the launch traced here: 887 us
  waiting for transfers between devices  585 us (66%)
  matrix products  144 us (16%)
  local copies, waits for them, and re-layouts  79.6 us (9%)
  starting transfers between devices  37.9 us (4%)
  other arithmetic  25.4 us (3%)
  between operations  14.1 us (2%)
    all_to_all x4, waiting for transfers between devices, coulomb_solve(): lax.all_to_all(field, 'plane', split_axis=2, concat_axis=1, tiled=True)  186 us
    all_to_all x4, waiting for transfers between devices, coulomb_solve(): lax.all_to_all(field, 'plane', split_axis=1, concat_axis=2, tiled=True)  160 us
    psum x1, waiting for transfers between devices, from_root(): return lax.psum(kept, axis)  123 us
    psum x1, waiting for transfers between devices, local(): summed = lax.psum(owner_terms[turn], 'band')  117 us
    dot_general x4, matrix products, coulomb_solve(): jnp.einsum('pxyz,xu->puyz', field, table, precision=HIGHEST) * kernel  28.7 us
    dot_general x4, matrix products, coulomb_solve(): field = jnp.einsum('pxyz,zw->pxyw', field, table, precision=HIGHEST)  26.4 us
    dot_general x4, matrix products, coulomb_solve(): return jnp.einsum('pxyz,yv->pxvz', field, table, precision=HIGHEST)  26.2 us
    dot_general x4, matrix products, coulomb_solve(): field = jnp.einsum('pxyz,zw->pxyw', density, table, precision=HIGHEST)  25.4 us
  transfers between devices with their start and end apart: 10, of which 10 were waited for; matrix products, arithmetic and copies ran while one was open for 19% of the time, Pallas kernels for 0%

commit v1 on v0

--- a/solution.py
+++ b/solution.py
@@ -75,7 +75,7 @@
     owner_terms = jnp.stack(owner_list)
     own_extra = jnp.zeros((PAIR,) + shape_tail, jnp.float32)
     for turn in range(ROUNDS):
-        summed = lax.psum(owner_terms[turn], "band")
+        summed = jnp.sum(lax.all_gather(owner_terms[turn], "band"), axis=0)
         owner_flag = (lax.axis_index("band") == turn).astype(jnp.float32)
         own_extra = own_extra + owner_flag * summed
     local_sum = local_sum.at[0:PAIR].add(own_extra)

time: 890 us -> 1080 us (1.21)
  waiting for transfers between devices: 585 us -> 755 us
  other arithmetic: 25.4 us -> 38.4 us
    all_gather x0 -> x4, waiting for transfers between devices: none -> 286 us  [local(): summed = jnp.sum(lax.all_gather(owner_terms[turn], 'band'), axis=0)]
    psum x1 -> x0, waiting for transfers between devices: 117 us -> none  [local(): summed = lax.psum(owner_terms[turn], 'band')]
    reduce_sum x0 -> x4, other arithmetic: none -> 13.3 us  [local(): summed = jnp.sum(lax.all_gather(owner_terms[turn], 'band'), axis=0)]
  transfers between devices with their start and end apart: 10 -> 13, of which waited for: 10 -> 13; matrix products, arithmetic and copies ran while one was open for 19% -> 17% of each run, Pallas kernels for 0% -> 0%
where the time goes in v1:
time: 1080 us; the launch traced here: 1070 us
  waiting for transfers between devices  755 us (70%)
  matrix products  144 us (13%)
  local copies, waits for them, and re-layouts  79.8 us (7%)
  other arithmetic  38.4 us (4%)
  starting transfers between devices  38.2 us (4%)
  between operations  14 us (1%)
    all_gather x4, waiting for transfers between devices, local(): summed = jnp.sum(lax.all_gather(owner_terms[turn], 'band'), axis=0)  286 us
    all_to_all x4, waiting for transfers between devices, coulomb_solve(): lax.all_to_all(field, 'plane', split_axis=2, concat_axis=1, tiled=True)  186 us
    all_to_all x4, waiting for transfers between devices, coulomb_solve(): lax.all_to_all(field, 'plane', split_axis=1, concat_axis=2, tiled=True)  160 us
    psum x1, waiting for transfers between devices, from_root(): return lax.psum(kept, axis)  123 us
    dot_general x4, matrix products, coulomb_solve(): jnp.einsum('pxyz,xu->puyz', field, table, precision=HIGHEST) * kernel  28.7 us
    dot_general x4, matrix products, coulomb_solve(): field = jnp.einsum('pxyz,zw->pxyw', field, table, precision=HIGHEST)  26.2 us
    dot_general x4, matrix products, coulomb_solve(): return jnp.einsum('pxyz,yv->pxvz', field, table, precision=HIGHEST)  26.2 us
    dot_general x4, matrix products, coulomb_solve(): field = jnp.einsum('pxyz,zw->pxyw', density, table, precision=HIGHEST)  25.4 us
  transfers between devices with their start and end apart: 13, of which 13 were waited for; matrix products, arithmetic and copies ran while one was open for 17% of the time, Pallas kernels for 0%

profile of v1, /device:TPU:8, one launch (start us, length us, event | category | flops | bytes accessed | tf_op | source)
XLA Modules:
  0.0 1070.1 jit_solution(8239067504499139061)
XLA Ops:
  16.1 122.6 %all-reduce.3.cloned.1.call-done = (f32[2,6,96,96]{3,2,0,1:T(8,128)}, f32[2,6,96,96]{3,2,0,1:T(8,128)}, f32[2,6,96,96]{3,2,0,1:T(8,128)}, f32[2,6,96,96]{3,2,0,1:T(8,128)}) async-done(((f32[2,6,96,96]{3,2,0,1:T(8,128)}, f32[2,6,96,96]{3,2,0,1:T(8,128)}, f32[2,6,96,96]{3,2,0,1:T(8,128)}, f32[2,6,96,96]{3,2,0,1:T(8,128)}), (f32[2,6,96,96]{3,2,0,1:T(8,128)}, f32[2,6,96,96]{3,2,0,1:T(8,128)}, ...) | async-done | bytes 1769488 | tf_op jit(solution)/shard_map/psum | solution.py:17
  138.8 9.3 broadcast_multiply_fusion.2
  148.1 6.3 fusion.52
  154.4 4.5 convolution_bitcast_fusion.1
  158.9 4.9 copy.143
  163.8 4.8 all-to-all-start.4
  168.7 6.3 fusion.55
  175.0 4.5 convolution_bitcast_fusion.2
  179.5 5.0 copy.133
  184.5 47.5 %all-to-all-done.4 = f32[16,6,96,96]{3,0,1,2:T(8,128)} async-done(((f32[16,6,96,96]{3,0,1,2:T(8,128)}), f32[16,6,96,96]{3,0,1,2:T(8,128)}, u32[]{:S(2)}, u32[]{:S(2)}) %all-to-all-start.4) | async-done | bytes 3538976 | tf_op jit(solution)/shard_map/all_to_all | solution.py:48
  232.0 5.2 all-to-all-start.2
  237.2 6.3 fusion.49
  243.5 4.5 convolution_bitcast_fusion
  248.0 4.9 copy.153
  253.0 47.7 %all-to-all-done.2 = f32[16,6,96,96]{3,0,1,2:T(8,128)} async-done(((f32[16,6,96,96]{3,0,1,2:T(8,128)}), f32[16,6,96,96]{3,0,1,2:T(8,128)}, u32[]{:S(2)}, u32[]{:S(2)}) %all-to-all-start.2) | async-done | bytes 3538976 | tf_op jit(solution)/shard_map/all_to_all | solution.py:48
  300.7 4.7 all-to-all-start.6
  305.4 6.3 fusion.58
  311.8 4.5 convolution_bitcast_fusion.3
  316.3 5.0 copy.123
  321.2 47.7 %all-to-all-done.6 = f32[16,6,96,96]{3,0,1,2:T(8,128)} async-done(((f32[16,6,96,96]{3,0,1,2:T(8,128)}), f32[16,6,96,96]{3,0,1,2:T(8,128)}, u32[]{:S(2)}, u32[]{:S(2)}) %all-to-all-start.6) | async-done | bytes 3538976 | tf_op jit(solution)/shard_map/all_to_all | solution.py:48
  368.9 5.0 all-to-all-start
  374.3 2.9 copy.145
  377.2 7.1 fusion.14
  384.3 4.7 fusion.38
  389.1 4.9 copy.147
  394.0 42.9 %all-to-all-done = f32[16,6,96,96]{3,0,1,2:T(8,128)} async-done(((f32[16,6,96,96]{3,0,1,2:T(8,128)}), f32[16,6,96,96]{3,0,1,2:T(8,128)}, u32[]{:S(2)}, u32[]{:S(2)}) %all-to-all-start) | async-done | bytes 3538976 | tf_op jit(solution)/shard_map/all_to_all | solution.py:48
  436.9 4.6 all-to-all-start.5
  441.5 2.9 copy.135
  444.4 7.1 fusion.18
  451.6 5.0 fusion.35
  456.5 5.0 copy.137
  461.5 43.5 %all-to-all-done.5 = f32[16,96,6,96]{3,0,2,1:T(8,128)} async-done(((f32[16,96,6,96]{3,0,2,1:T(8,128)}), f32[16,96,6,96]{3,0,2,1:T(8,128)}, u32[]{:S(2)}, u32[]{:S(2)}) %all-to-all-start.5) | async-done | bytes 3538976 | tf_op jit(solution)/shard_map/all_to_all | solution.py:51
  505.0 4.6 all-to-all-start.3
  509.6 2.9 copy.155
  512.5 7.1 fusion.10
  519.6 4.7 fusion.41
  524.4 4.9 copy.157
  529.2 43.8 %all-to-all-done.3 = f32[16,96,6,96]{3,0,2,1:T(8,128)} async-done(((f32[16,96,6,96]{3,0,2,1:T(8,128)}), f32[16,96,6,96]{3,0,2,1:T(8,128)}, u32[]{:S(2)}, u32[]{:S(2)}) %all-to-all-start.3) | async-done | bytes 3538976 | tf_op jit(solution)/shard_map/all_to_all | solution.py:51
  573.0 4.6 all-to-all-start.7
  580.6 7.4 fusion.22
  588.0 5.3 fusion.32
  593.3 5.0 copy.127
  598.3 42.9 %all-to-all-done.7 = f32[16,96,6,96]{3,0,2,1:T(8,128)} async-done(((f32[16,96,6,96]{3,0,2,1:T(8,128)}), f32[16,96,6,96]{3,0,2,1:T(8,128)}, u32[]{:S(2)}, u32[]{:S(2)}) %all-to-all-start.7) | async-done | bytes 3538976 | tf_op jit(solution)/shard_map/all_to_all | solution.py:51
  641.2 4.6 all-to-all-start.1
  658.9 6.9 fusion.12
  665.8 6.9 fusion.16
  672.7 7.1 fusion.8
  679.8 29.5 %all-to-all-done.1 = f32[16,96,6,96]{3,0,2,1:T(8,128)} async-done(((f32[16,96,6,96]{3,0,2,1:T(8,128)}), f32[16,96,6,96]{3,0,2,1:T(8,128)}, u32[]{:S(2)}, u32[]{:S(2)}) %all-to-all-start.1) | async-done | bytes 3538976 | tf_op jit(solution)/shard_map/all_to_all | solution.py:51
  709.2 2.9 copy.128
  712.2 5.4 fusion.20
  717.6 6.3 multiply_reduce_fusion.6
  724.0 6.5 multiply_reduce_fusion.5
  730.6 6.5 multiply_reduce_fusion.4
  737.1 6.8 multiply_reduce_fusion.7
  743.9 5.2 multiply_reduce_fusion.3
  751.1 4.9 add_add_fusion
  756.0 67.3 %all-gather.9.cloned.1.call-done = f32[16,6,96,96]{3,2,1,0:T(8,128)} async-done(((f32[2,6,96,96]{3,2,1,0:T(8,128)}), f32[16,6,96,96]{3,2,1,0:T(8,128)}) %all-gather.9.cloned.1.call-update) | async-done | bytes 3538960 | tf_op jit(solution)/shard_map/all_gather | solution.py:78
  823.3 2.9 reduce_sum.113
  826.2 73.1 %all-gather.11.cloned.1.call-done = f32[16,6,96,96]{3,2,1,0:T(8,128)} async-done(((f32[2,6,96,96]{3,2,1,0:T(8,128)}), f32[16,6,96,96]{3,2,1,0:T(8,128)}) %all-gather.11.cloned.1.call-update) | async-done | bytes 3538960 | tf_op jit(solution)/shard_map/all_gather | solution.py:78
  899.4 2.9 reduce_sum.115
  902.3 73.0 %all-gather.13.cloned.1.call-done = f32[16,6,96,96]{3,2,1,0:T(8,128)} async-done(((f32[2,6,96,96]{3,2,1,0:T(8,128)}), f32[16,6,96,96]{3,2,1,0:T(8,128)}) %all-gather.13.cloned.1.call-update) | async-done | bytes 3538960 | tf_op jit(solution)/shard_map/all_gather | solution.py:78
  975.3 3.7 reduce_sum.117
  979.0 72.1 %all-gather.15.cloned.1.call-done = f32[16,6,96,96]{3,2,1,0:T(8,128)} async-done(((f32[2,6,96,96]{3,2,1,0:T(8,128)}), f32[16,6,96,96]{3,2,1,0:T(8,128)}) %all-gather.15.cloned.1.call-update) | async-done | bytes 3538960 | tf_op jit(solution)/shard_map/all_gather | solution.py:78
  1051.1 3.7 reduce_sum.119
  (57 shorter events, 36.2 us)
Async XLA Ops:
  6.5 132.2 %all-reduce.3.cloned.1.call-start = ((), (), s32[]{:S(2)}) async-start(), calls=%async_computation.12 | async-start | bytes 4718592 | tf_op jit(solution)/shard_map/psum | solution.py:17
  163.8 68.1 %all-to-all-start.4 = ((f32[16,6,96,96]{3,0,1,2:T(8,128)}), f32[16,6,96,96]{3,0,1,2:T(8,128)}, u32[]{:S(2)}, u32[]{:S(2)}) async-start(f32[16,6,96,96]{3,0,1,2:T(8,128)} %copy.143), calls=%async_computation.4 | async-start | bytes 9437184 | tf_op jit(solution)/shard_map/all_to_all | solution.py:48
  232.0 68.7 %all-to-all-start.2 = ((f32[16,6,96,96]{3,0,1,2:T(8,128)}), f32[16,6,96,96]{3,0,1,2:T(8,128)}, u32[]{:S(2)}, u32[]{:S(2)}) async-start(f32[16,6,96,96]{3,0,1,2:T(8,128)} %copy.133), calls=%async_computation.2 | async-start | bytes 9437184 | tf_op jit(solution)/shard_map/all_to_all | solution.py:48
  300.7 68.2 %all-to-all-start.6 = ((f32[16,6,96,96]{3,0,1,2:T(8,128)}), f32[16,6,96,96]{3,0,1,2:T(8,128)}, u32[]{:S(2)}, u32[]{:S(2)}) async-start(f32[16,6,96,96]{3,0,1,2:T(8,128)} %copy.153), calls=%async_computation.6 | async-start | bytes 9437184 | tf_op jit(solution)/shard_map/all_to_all | solution.py:48
  368.9 68.1 %all-to-all-start = ((f32[16,6,96,96]{3,0,1,2:T(8,128)}), f32[16,6,96,96]{3,0,1,2:T(8,128)}, u32[]{:S(2)}, u32[]{:S(2)}) async-start(f32[16,6,96,96]{3,0,1,2:T(8,128)} %copy.123), calls=%async_computation | async-start | bytes 9437184 | tf_op jit(solution)/shard_map/all_to_all | solution.py:48
  436.9 68.1 %all-to-all-start.5 = ((f32[16,96,6,96]{3,0,2,1:T(8,128)}), f32[16,96,6,96]{3,0,2,1:T(8,128)}, u32[]{:S(2)}, u32[]{:S(2)}) async-start(f32[16,96,6,96]{3,0,2,1:T(8,128)} %copy.147), calls=%async_computation.5 | async-start | bytes 9437184 | tf_op jit(solution)/shard_map/all_to_all | solution.py:51
  505.0 68.0 %all-to-all-start.3 = ((f32[16,96,6,96]{3,0,2,1:T(8,128)}), f32[16,96,6,96]{3,0,2,1:T(8,128)}, u32[]{:S(2)}, u32[]{:S(2)}) async-start(f32[16,96,6,96]{3,0,2,1:T(8,128)} %copy.137), calls=%async_computation.3 | async-start | bytes 9437184 | tf_op jit(solution)/shard_map/all_to_all | solution.py:51
  573.0 68.1 %all-to-all-start.7 = ((f32[16,96,6,96]{3,0,2,1:T(8,128)}), f32[16,96,6,96]{3,0,2,1:T(8,128)}, u32[]{:S(2)}, u32[]{:S(2)}) async-start(f32[16,96,6,96]{3,0,2,1:T(8,128)} %copy.157), calls=%async_computation.7 | async-start | bytes 9437184 | tf_op jit(solution)/shard_map/all_to_all | solution.py:51
  598.2 51.4 %copy-start.1 = (f32[2,6,96,96]{3,2,0,1:T(8,128)S(1)}, f32[2,6,96,96]{3,2,0,1:T(8,128)}, u32[]{:S(2)}) copy-start(f32[2,6,96,96]{3,2,0,1:T(8,128)} %get-tuple-element.23) | copy-start | bytes 1327108
  598.2 52.2 %copy-start = (f32[2,6,96,96]{3,2,0,1:T(8,128)S(1)}, f32[2,6,96,96]{3,2,0,1:T(8,128)}, u32[]{:S(2)}) copy-start(f32[2,6,96,96]{3,2,0,1:T(8,128)} %get-tuple-element.24) | copy-start | bytes 1327108
  641.2 68.1 %all-to-all-start.1 = ((f32[16,96,6,96]{3,0,2,1:T(8,128)}), f32[16,96,6,96]{3,0,2,1:T(8,128)}, u32[]{:S(2)}, u32[]{:S(2)}) async-start(f32[16,96,6,96]{3,0,2,1:T(8,128)} %copy.127), calls=%async_computation.1 | async-start | bytes 9437184 | tf_op jit(solution)/shard_map/all_to_all | solution.py:51
  645.7 177.6 %all-gather.9.cloned.1.call-start = ((), (), s32[]{:S(2)}) async-start(), calls=%async_computation.8 | async-start | bytes 5308416 | tf_op jit(solution)/shard_map/all_gather | solution.py:78
  709.2 8.4 slice-start.4
  712.2 5.4 slice-start.5
  712.2 11.8 %slice-start.2 = ((s8[4718592]{0:T(1024)(128)(4,1)}), s8[4194304]{0:T(1024)(128)(4,1)S(1)}, s32[]{:S(2)}) async-start(s8[4718592]{0:T(1024)(128)(4,1)} %bitcast.185), calls=%async_computation.15 | async-start | bytes 8388608
  717.6 6.4 slice-start.3
  717.6 6.3 copy-start.4
  717.6 12.9 %slice-start = ((s8[4718592]{0:T(1024)(128)(4,1)}), s8[4194304]{0:T(1024)(128)(4,1)S(1)}, s32[]{:S(2)}) async-start(s8[4718592]{0:T(1024)(128)(4,1)} %bitcast.183), calls=%async_computation.13 | async-start | bytes 8388608
  724.0 6.6 slice-start.1
  724.0 6.6 copy-start.3
  730.6 6.6 copy-start.2
  749.1 150.2 %all-gather.11.cloned.1.call-start = ((), (), s32[]{:S(2)}) async-start(), calls=%async_computation.9 | async-start | bytes 5308416 | tf_op jit(solution)/shard_map/all_gather | solution.py:78
  749.9 225.4 %all-gather.13.cloned.1.call-start = ((), (), s32[]{:S(2)}) async-start(), calls=%async_computation.10 | async-start | bytes 5308416 | tf_op jit(solution)/shard_map/all_gather | solution.py:78
  750.4 300.7 %all-gather.15.cloned.1.call-start = ((), (), s32[]{:S(2)}) async-start(), calls=%async_computation.11 | async-start | bytes 5308416 | tf_op jit(solution)/shard_map/all_gather | solution.py:78
Sparse Core Ops, SparseCore 0:
  13.8 124.9 all-reduce.2
  749.2 74.0 all-gather.8
  825.6 73.6 all-gather.10
  901.5 73.6 all-gather.12
  977.4 73.6 all-gather.14
